TPU v7x, 256 devices: a whole 4x4x8 slice. The times are simulated.
256 devices in a mesh: tm: 16 (over x, y_lo, core), batch: 16 (over z, y_hi).
Axes of the slice: x: 4, y: 4 (y_hi: 2, y_lo: 2; y = y_hi * 2 + y_lo), z: 8, core: 2. Of those that a mesh axis runs over, the one named last changes fastest.
Arguments:
- signal: bfloat16 [16, 2048, 4096], P('batch', 'tm'), may hold values from -7.5 to 7.5
- gate_input: bfloat16 [16, 2048, 4096], P('batch', 'tm'), may hold values from -6 to 6
- bc_forward: bfloat16 [16, 2048, 128], P('batch', 'tm'), may hold values from -6 to 6
- bc_backward: bfloat16 [16, 2048, 128], P('batch', 'tm'), may hold values from -6 to 6
- step_raw: bfloat16 [16, 2048, 128], P('batch', 'tm'), may hold values from -12 to 2
- decay_rate: float32 [2, 64], replicated, may hold values from 0.3 to 1
- conv_weight: float32 [2, 4, 4224], replicated, may hold values from -3 to 3
- conv_bias: float32 [2, 4224], replicated, may hold values from -1.5 to 1.5
- skip_gain: float32 [2, 64], replicated, may hold values from 0.5 to 1.5
- norm_gain: float32 [4096], replicated, may hold values from 0.1 to 1.9
Outputs:
- mixed: bfloat16 [16, 2048, 4096], P(None, 'batch', 'tm')
All inputs are finite; a program needn't handle non-finite values.
Results may differ from a plain program's by a relative error of at most 0.0075.
Values may be sent and summed in bfloat16 or wider, within the bound.
No kernel may reach another device: no remote copies, remote signals or barrier semaphores. Data moves between devices by JAX's collectives and lax.ppermute only.
A program may use at most 256 MiB of HBM per device.

v0:
```python
import jax
import jax.numpy as jnp
from jax import lax
from jax.experimental import pallas as pl
from jax.experimental.pallas import tpu as pltpu
from jax.sharding import PartitionSpec as P


INNER = 4096
HEADDIM = 64
STATE = 64
GROUP = 128
HEADS = 64
BLOCKS = 16
OWN = 4
WIDE = OWN * HEADDIM
HALF = GROUP // 2
ROWS = GROUP + HALF + 8
EARLY, LATE = (2,), (0, 1, 3)
EPSILON = 1e-05
UNROLL_BC, UNROLL_X, UNROLL_Y = 8, 8, 4
LOG2E = 1.4426950408889634
VMEM = pl.BlockSpec(memory_space=pltpu.VMEM)
LIMIT = pltpu.CompilerParams(vmem_limit_bytes=32 << 20)
ANY = pl.BlockSpec(memory_space=pl.ANY)
SMEM = pl.BlockSpec(memory_space=pltpu.SMEM)


def pack_kernel(signal, bcf, bcb, step, out, buf, bc, steps, came, small, sent):
    def fetch(c):
        source = signal.at[0, :, pl.ds(c * WIDE, WIDE)]
        return pltpu.make_async_copy(source, buf.at[c, pl.ds(0, GROUP)], came.at[c])

    def send(c):
        return pltpu.make_async_copy(buf.at[c], out.at[c], sent.at[c])

    sides = [
        pltpu.make_async_copy(step.at[0], steps, small.at[0]),
        pltpu.make_async_copy(bcf.at[0], bc.at[0], small.at[1]),
        pltpu.make_async_copy(bcb.at[0], bc.at[1], small.at[2]),
    ]
    for side in sides:
        side.start()
    for c in range(BLOCKS):
        fetch(c).start()
    for side in sides:
        side.wait()
    folded = [jnp.concatenate([bc[d, :HALF], bc[d, HALF:]], axis=1) for d in range(2)]
    turned = steps[...].astype(jnp.float32).T
    for c in range(BLOCKS):
        buf[c, GROUP : GROUP + HALF] = folded[c % 2]
        mine = jnp.concatenate(
            [turned[c * OWN : (c + 1) * OWN], turned[HEADS + c * OWN : HEADS + (c + 1) * OWN]], axis=0
        )
        buf[c, GROUP + HALF :] = jnp.concatenate([mine, jnp.zeros_like(mine)], axis=1).astype(
            jnp.bfloat16
        )
    for c in range(BLOCKS):
        fetch(c).wait()
        send(c).start()
    for c in range(BLOCKS):
        send(c).wait()


def half_silu(h):
    return h + h * jnp.tanh(h)


def pieces(value):
    parts = []
    for _ in range(3):
        part = value.astype(jnp.bfloat16).astype(jnp.float32)
        parts.append(part)
        value = value - part
    return parts


def ssm_kernel(
    buf, other, cw, cb, rate, skip, y, ybuf, sent, raw, row_s, cum_s, dec_s, end_s, tot_s, fixed_s, x_s, c_s, bt_s, btb_s, st_s, carry_s
):
    f32, bf16 = jnp.float32, jnp.bfloat16
    tm = lax.axis_index("tm")
    n8 = BLOCKS * 8

    raw_steps = buf[:, GROUP + HALF :, :GROUP].astype(f32).reshape(n8, GROUP)
    z = jnp.exp(-jnp.abs(raw_steps))
    u = 1.0 + z
    log1p = jnp.where(u == 1.0, z, jnp.log(u) * (z / jnp.where(u == 1.0, 1.0, u - 1.0)))
    dt = jnp.maximum(raw_steps, 0.0) + log1p
    sub = lax.broadcasted_iota(jnp.int32, (8, GROUP), 0)
    rates = jnp.zeros((8, GROUP), f32)
    for k in range(8):
        rates = jnp.where(sub == k, rate[k // OWN, tm * OWN + k % OWN], rates)
    decay = (dt.reshape(BLOCKS, 8, GROUP) * (rates * (-LOG2E))[None]).reshape(n8, GROUP)
    ri = lax.broadcasted_iota(jnp.int32, (GROUP, GROUP), 0)
    ci = lax.broadcasted_iota(jnp.int32, (GROUP, GROUP), 1)
    sums = jnp.concatenate([(ri <= ci).astype(f32), (ri >= ci).astype(f32)], axis=1).astype(bf16)
    both = jnp.dot(
        jnp.concatenate(pieces(decay), axis=1).astype(bf16),
        jnp.concatenate([sums] * 3, axis=0),
        preferred_element_type=f32,
    )
    prefix, suffix = both[:, :GROUP], both[:, GROUP:]
    is_fwd = lax.broadcasted_iota(jnp.int32, (n8, GROUP), 0) % 8 < OWN
    cum = jnp.where(is_fwd, prefix, suffix)
    total = jnp.where(is_fwd[:, :1], prefix[:, GROUP - 1 :], suffix[:, :1])
    row = cum - jnp.log(dt) * LOG2E
    row_s[...] = -row
    cum_s[...] = cum
    dec_s[...] = jnp.exp2(cum)
    end_s[...] = jnp.exp2(total - row)
    tot_s[...] = jnp.broadcast_to(jnp.exp2(total), (n8, GROUP))

    low = lax.broadcasted_iota(jnp.int32, (GROUP, 128), 1) < HEADDIM
    sub128 = lax.broadcasted_iota(jnp.int32, (96, 128), 0)
    for k in range(12):
        if k < 8:
            chosen = (sub128 < 24) & (sub128 % 8 == k)
        else:
            d, p = divmod(k - 8, 2)
            head = d * OWN + 2 * p + jnp.where(low[:96], 0, 1)
            chosen = (sub128 >= 32) & (sub128 < 56) & (sub128 % 8 == head)
        fixed_s[k] = jnp.where(chosen, 1.0, 0.0).astype(bf16)

    for t in range(4):
        raw[t, 0:8] = jnp.zeros((8, 128), f32)
        raw[t, 8 + BLOCKS * GROUP :] = jnp.zeros((8, 128), f32)

    even = lax.rem(tm, 2) == 0

    def widen(i, _):
        at = pl.multiple_of(8 + i * GROUP, 8)
        for t in range(2):
            raw[t, pl.ds(at, GROUP)] = buf[i, :GROUP, t * 128 : (t + 1) * 128].astype(f32)
            near = buf[i, GROUP : GROUP + HALF, t * 128 : (t + 1) * 128].astype(f32)
            far = other[i, :, t * 128 : (t + 1) * 128].astype(f32)
            raw[2, pl.ds(at + t * HALF, HALF)] = jnp.where(even, near, far)
            raw[3, pl.ds(at + t * HALF, HALF)] = jnp.where(even, far, near)
        return 0

    lax.fori_loop(0, BLOCKS, widen, 0)

    def conv(t, i, d, taps, offset):
        sign = 1 if d == 0 else -1
        acc = offset
        for k in range(4):
            acc = acc + taps[k] * raw[t, pl.ds(i * GROUP + (8 + sign * (k - 3)), GROUP)]
        return half_silu(acc)

    def taps_of(d, lanes):
        return [cw[d, pl.ds(k, 1), lanes] * 0.5 for k in range(4)], cb[pl.ds(d, 1), lanes] * 0.5

    for d in range(2):
        taps, offset = taps_of(d, slice(INNER, INNER + 128))

        def convolve_bc(j, _):
            for e in range(UNROLL_BC):
                i = j * UNROLL_BC + e
                bc = conv(2 + d, i, d, taps, offset).astype(bf16).astype(f32)
                c_s[d, i] = jnp.where(low, pltpu.roll(bc, STATE, 1), bc).astype(bf16)
                turned = bc.T[:STATE]
                bt_s[d, i] = turned
                btb_s[d, i] = turned.astype(bf16)
            return 0

        lax.fori_loop(0, BLOCKS // UNROLL_BC, convolve_bc, 0)

    for p in range(OWN // 2):
        lanes = pl.ds(pl.multiple_of(tm * WIDE + p * 128, 128), 128)
        filters = [taps_of(d, lanes) for d in range(2)]

        def convolve(j, _):
            for e in range(UNROLL_X):
                i = j * UNROLL_X + e
                ends = end_s[pl.ds(pl.multiple_of(8 * i, 8), 8)]
                for d in range(2):
                    x = conv(p, i, d, *filters[d]).astype(bf16)
                    x_s[d, p, i] = x
                    k = d * OWN + 2 * p
                    turned = bt_s[d, i]
                    scaled = jnp.concatenate(
                        [turned * ends[k : k + 1], turned * ends[k + 1 : k + 2]], axis=0
                    ).astype(bf16)
                    state = jnp.dot(scaled, x, preferred_element_type=f32)
                    st_s[d, p, i] = jnp.where(low[:STATE], state[:STATE], state[STATE:])
            return 0

        lax.fori_loop(0, BLOCKS // UNROLL_X, convolve, 0)

    def scan(i, carries):
        new = []
        for d in range(2):
            at = i if d == 0 else BLOCKS - 1 - i
            rows = tot_s[pl.ds(pl.multiple_of(8 * at, 8), 8)]
            for p in range(OWN // 2):
                carry = carries[2 * d + p]
                high = carry.astype(bf16)
                lanes = slice(p * 128, (p + 1) * 128)
                carry_s[d, at, :STATE, lanes] = high
                carry_s[d, at, STATE:, lanes] = (carry - high.astype(f32)).astype(bf16)
                k = d * OWN + 2 * p
                keep = jnp.where(low[:1], rows[k : k + 1], rows[k + 1 : k + 2])
                new.append(keep * carry + st_s[d, p, at])
        return tuple(new)

    lax.fori_loop(0, BLOCKS, scan, tuple(jnp.zeros((STATE, 128), f32) for _ in range(4)))

    skips = []
    for d in range(2):
        for p in range(OWN // 2):
            at = tm * OWN + 2 * p
            skips.append(jnp.where(low[:1], skip[d, at], skip[d, at + 1]))
    sub32 = lax.broadcasted_iota(jnp.int32, (32, GROUP), 0)
    ones = jnp.where(sub32 < 24, 1.0, 0.0)
    blank = jnp.zeros((8, GROUP), f32)

    def one_block(i):
        at = pl.ds(pl.multiple_of(8 * i, 8), 8)
        left = jnp.concatenate(
            [ones, *pieces(cum_s[at]), blank, *pieces(dec_s[at]), blank, jnp.zeros((32, GROUP), f32)],
            axis=0,
        ).T.astype(bf16)
        rows = jnp.concatenate([*pieces(row_s[at]), blank], axis=0)
        right = []
        for k in range(12):
            part = jnp.where(sub32 % 8 == k, rows, 0.0) if k < 8 else jnp.zeros((32, GROUP), f32)
            right.append(jnp.concatenate([part.astype(bf16), fixed_s[k]], axis=0))
        grid = jnp.dot(left, jnp.concatenate(right, axis=1), preferred_element_type=f32)
        scores, wide = [], [0.0, 0.0]
        for d in range(2):
            c = c_s[d, i]
            score = jnp.dot(c[:, :STATE], btb_s[d, i], preferred_element_type=f32)
            scores.append(jnp.where((ri >= ci) if d == 0 else (ri <= ci), score, 0.0))
            carried = jnp.dot(c, carry_s[d, i], preferred_element_type=f32)
            for p in range(OWN // 2):
                lanes = slice(p * 128, (p + 1) * 128)
                decays = grid[:, (8 + 2 * d + p) * 128 : (9 + 2 * d + p) * 128]
                wide[p] = (
                    wide[p] + carried[:, lanes] * decays + skips[2 * d + p] * x_s[d, p, i].astype(f32)
                )
        for p in range(OWN // 2):
            heads = []
            for q in range(2):
                parts = []
                for d in range(2):
                    k = d * OWN + 2 * p + q
                    grow = jnp.exp2(jnp.minimum(grid[:, k * 128 : (k + 1) * 128], 64.0))
                    parts.append((grow * scores[d]).astype(bf16))
                heads.append(jnp.concatenate(parts, axis=1))
            local = jnp.dot(
                jnp.concatenate(heads, axis=0),
                jnp.concatenate([x_s[0, p, i], x_s[1, p, i]], axis=0),
                preferred_element_type=f32,
            )
            local = jnp.where(low, local[:GROUP], local[GROUP:])
            ybuf[i, :, p * 128 : (p + 1) * 128] = local + wide[p]

    def send(j):
        at = pl.ds(j * UNROLL_Y, UNROLL_Y)
        return pltpu.make_async_copy(ybuf.at[at], y.at[at], sent.at[j])

    def outputs(j, _):
        @pl.when(j > 0)
        def _():
            send(j - 1).start()

        for e in range(UNROLL_Y):
            one_block(j * UNROLL_Y + e)
        return 0

    count = BLOCKS // UNROLL_Y
    lax.fori_loop(0, count, outputs, 0)
    send(count - 1).start()
    for j in range(count):
        send(j).wait()


def gate_kernel(y, gate, gated, sums, out, wide, ybuf, came, sent):
    f32, bf16 = jnp.float32, jnp.bfloat16

    def fetch(j):
        at = pl.ds(j * 4, 4)
        return pltpu.make_async_copy(y.at[at], ybuf.at[at], came.at[j])

    def send(j):
        at = pl.ds(j * 4, 4)
        return pltpu.make_async_copy(out.at[at], gated.at[at], sent.at[j])

    for j in range(BLOCKS // 4):
        fetch(j).start()

    def four(j, _):
        @pl.when(j > 0)
        def _():
            send(j - 1).start()

        for e in range(4):
            i = j * 4 + e
            wide[i] = half_silu(gate[i].astype(f32) * 0.5)
        fetch(j).wait()
        for e in range(4):
            i = j * 4 + e
            g = ybuf[i] * wide[i]
            out[i] = g.astype(bf16)
            square = g * g
            square = square[:, :128] + square[:, 128:]
            high = square.astype(bf16)
            parts = jnp.concatenate([high, (square - high.astype(f32)).astype(bf16)], axis=1)
            total = lax.dot_general(
                jnp.ones((8, WIDE), bf16), parts, (((1,), (1,)), ((), ())), preferred_element_type=f32
            )
            sums[pl.ds(i, 1)] = total[:1]
        return 0

    lax.fori_loop(0, BLOCKS // 4, four, 0)
    send(BLOCKS // 4 - 1).start()
    for j in range(BLOCKS // 4):
        send(j).wait()


def norm_kernel(gated, total, gain, target, out, sent):
    gains = gain[0:1, pl.ds(pl.multiple_of(lax.axis_index("tm") * WIDE, WIDE), WIDE)]
    inv = lax.rsqrt(total[...] * (1.0 / INNER) + EPSILON)
    columns = jnp.concatenate([inv, jnp.zeros((GROUP - BLOCKS, GROUP), jnp.float32)], axis=0).T

    def send(j):
        at = pl.ds(j * 4, 4)
        return pltpu.make_async_copy(out.at[at], target.at[at], sent.at[j])

    for j in range(BLOCKS // 4):
        if j > 0:
            send(j - 1).start()
        for i in range(4 * j, 4 * j + 4):
            wide = gated[i].astype(jnp.float32) * columns[:, i : i + 1] * gains
            out[i] = wide.astype(jnp.bfloat16)
    send(BLOCKS // 4 - 1).start()
    for j in range(BLOCKS // 4):
        send(j).wait()


def total_of(sums):
    for moves in (
        [[i ^ b for i in range(BLOCKS)] for b in (1, 2, 3)],
        [[(i + b) % BLOCKS for i in range(BLOCKS)] for b in (4, 8, 12)],
    ):
        came = [lax.ppermute(sums, "tm", list(enumerate(move))) for move in moves]
        sums = sums + came[0] + came[1] + came[2]
    return sums


def turned_over(rows, bits):
    mine = lax.axis_index("batch")
    for b in bits:
        pairs = rows.reshape(BLOCKS >> (b + 1), 2, 1 << b, GROUP)
        upper = (mine >> b) & 1 == 1
        give = jnp.where(upper, pairs[:, 0], pairs[:, 1])
        got = lax.ppermute(give, "batch", [(i, i ^ (1 << b)) for i in range(BLOCKS)])
        pairs = [jnp.where(upper, got, pairs[:, 0]), jnp.where(upper, pairs[:, 1], got)]
        rows = jnp.stack(pairs, axis=1).reshape(BLOCKS, GROUP)
    return rows


def far(array):
    return pltpu.with_memory_space_constraint(array, pltpu.HBM)


def local(array):
    return pltpu.with_memory_space_constraint(array, pltpu.VMEM)


def swap(array, axis):
    return lax.all_to_all(array, axis, split_axis=0, concat_axis=0, tiled=True)


def shards(
    signal,
    gate_input,
    bc_forward,
    bc_backward,
    step_raw,
    decay_rate,
    conv_weight,
    conv_bias,
    skip_gain,
    norm_gain,
):
    f32, bf16 = jnp.float32, jnp.bfloat16
    packed = pl.pallas_call(
        pack_kernel,
        out_shape=pltpu.HBM((BLOCKS, ROWS, WIDE), bf16),
        in_specs=[ANY] * 4,
        out_specs=ANY,
        scratch_shapes=[
            pltpu.VMEM((BLOCKS, ROWS, WIDE), bf16),
            pltpu.VMEM((2, GROUP, 128), bf16),
            pltpu.VMEM((GROUP, 128), bf16),
            pltpu.SemaphoreType.DMA((BLOCKS,)),
            pltpu.SemaphoreType.DMA((3,)),
            pltpu.SemaphoreType.DMA((BLOCKS,)),
        ],
        name="pack",
        cost_estimate=pl.CostEstimate(flops=0, bytes_accessed=3 << 20, transcendentals=0),
    )(*[far(a) for a in (signal, bc_forward, bc_backward, step_raw)])
    gates = gate_input[0].reshape(GROUP, BLOCKS, WIDE).transpose(1, 0, 2)
    got, gates = lax.optimization_barrier((swap(packed, "tm"), gates))
    other = lax.ppermute(
        got[:, GROUP : GROUP + HALF], "tm", [(i, i ^ 1) for i in range(BLOCKS)]
    )
    gates = swap(gates, "tm")
    y = pl.pallas_call(
        ssm_kernel,
        out_shape=pltpu.HBM((BLOCKS, GROUP, WIDE), f32),
        compiler_params=LIMIT,
        in_specs=[VMEM, VMEM, VMEM, VMEM, SMEM, SMEM],
        out_specs=ANY,
        scratch_shapes=[
            pltpu.VMEM((BLOCKS, GROUP, WIDE), f32),
            pltpu.SemaphoreType.DMA((BLOCKS // UNROLL_Y,)),
            pltpu.VMEM((4, BLOCKS * GROUP + 16, 128), f32),
            *[pltpu.VMEM((BLOCKS * 8, GROUP), f32)] * 5,
            pltpu.VMEM((12, 96, 128), bf16),
            pltpu.VMEM((2, 2, BLOCKS, GROUP, 128), bf16),
            pltpu.VMEM((2, BLOCKS, GROUP, 128), bf16),
            pltpu.VMEM((2, BLOCKS, STATE, 128), f32),
            pltpu.VMEM((2, BLOCKS, STATE, 128), bf16),
            pltpu.VMEM((2, 2, BLOCKS, STATE, 128), f32),
            pltpu.VMEM((2, BLOCKS, 2 * STATE, WIDE), bf16),
        ],
        name="ssm",
        cost_estimate=pl.CostEstimate(
            flops=20_000_000_000, bytes_accessed=8 << 20, transcendentals=4_000_000
        ),
    )(local(got), local(other), conv_weight, conv_bias, decay_rate, skip_gain)
    gated, sums = pl.pallas_call(
        gate_kernel,
        out_shape=(
            pltpu.HBM((BLOCKS, GROUP, WIDE), bf16),
            pltpu.VMEM((BLOCKS, GROUP), f32),
        ),
        compiler_params=LIMIT,
        in_specs=[ANY, VMEM],
        out_specs=(ANY, VMEM),
        scratch_shapes=[
            pltpu.VMEM((BLOCKS, GROUP, WIDE), bf16),
            pltpu.VMEM((BLOCKS, GROUP, WIDE), f32),
            pltpu.VMEM((BLOCKS, GROUP, WIDE), f32),
            pltpu.SemaphoreType.DMA((BLOCKS // 4,)),
            pltpu.SemaphoreType.DMA((BLOCKS // 4,)),
        ],
        name="gate",
    )(far(y), local(gates))
    sums = turned_over(sums, EARLY)
    gated = swap(gated, "batch")
    sums = total_of(sums)
    sums = turned_over(sums, LATE)
    return pl.pallas_call(
        norm_kernel,
        out_shape=pltpu.HBM((BLOCKS, GROUP, WIDE), bf16),
        in_specs=[VMEM] * 3,
        out_specs=ANY,
        scratch_shapes=[
            pltpu.VMEM((BLOCKS, GROUP, WIDE), bf16),
            pltpu.SemaphoreType.DMA((BLOCKS // 4,)),
        ],
        compiler_params=LIMIT,
        name="norm",
    )(local(gated), sums, norm_gain[None])


def solution(mesh):
    in_specs = (
        P("batch", "tm", None),
        P("batch", "tm", None),
        P("batch", "tm", None),
        P("batch", "tm", None),
        P("batch", "tm", None),
        P(),
        P(),
        P(),
        P(),
        P(),
    )
    out_specs = P(None, "batch", "tm")
    return jax.shard_map(shards, mesh=mesh, in_specs=in_specs, out_specs=out_specs, check_vma=False)
```

profile of v0, /device:TPU:2, one launch (start us, length us, event | category | flops | bytes accessed | tf_op | source)
XLA Modules:
  0.0 110.7 jit_solution(15613761932787438076)
XLA Ops:
  0.0 2.8 %pack.1 = bf16[16,200,256]{2,1,0:T(8,128)(2,1)} custom-call(bf16[1,128,4096]{2,1,0:T(8,128)(2,1)} %signal.1, bf16[1,128,128]{2,1,0:T(8,128)(2,1)} %bcf.1, bf16[1,128,128]{2,1,0:T(8,128)(2,1)} %bcb.1, bf16[1,128,128]{2,1,0:T(8,128)(2,1)} %step.1), custom_call_target="tpu_custom_call" | custom-call | bytes 3145728 | tf_op jit(solution)/shard_map/pack/pallas_call | solution.py:388
  2.8 5.9 %all-to-all-start = ((bf16[16,200,256]{2,1,0:T(8,128)(2,1)}), bf16[16,200,256]{2,1,0:T(8,128)(2,1)S(1)}, u32[]{:S(2)}, u32[]{:S(2)}) async-start(bf16[16,200,256]{2,1,0:T(8,128)(2,1)} %pack.1), calls=%async_computation | async-start | bytes 3276800 | tf_op jit(solution)/shard_map/all_to_all | solution.py:372
  8.7 1.6 %copy.20 = bf16[1,128,4096]{1,2,0:T(8,128)(2,1)S(1)} copy(bf16[1,128,4096]{2,1,0:T(8,128)(2,1)} %param.11) | data formatting | bytes 2097152 | tf_op args[1]
  10.3 1.3 %copy.21 = bf16[128,16,256]{2,0,1:T(8,128)(2,1)} copy(bf16[128,16,256]{0,2,1:T(8,128)(2,1)S(1)} %bitcast.68) | data formatting | bytes 2097152 | tf_op jit(solution)/shard_map/reshape;squeeze | solution.py:404
  11.6 0.0 copy-start.1
  11.6 0.0 copy-start.2
  11.6 0.0 copy-start.3
  11.6 0.0 copy-start.4
  11.6 18.0 %all-to-all-done.buf = bf16[16,200,256]{2,1,0:T(8,128)(2,1)S(1)} async-done(((bf16[16,200,256]{2,1,0:T(8,128)(2,1)}), bf16[16,200,256]{2,1,0:T(8,128)(2,1)S(1)}, u32[]{:S(2)}, u32[]{:S(2)}) %all-to-all-start) | async-done | bytes 1638432 | tf_op jit(solution)/shard_map/all_to_all | solution.py:372
  29.7 0.9 slice.35
  30.5 0.0 collective-permute-start
  30.5 6.3 %all-to-all-start.1 = ((bf16[16,128,256]{2,1,0:T(8,128)(2,1)}), bf16[16,128,256]{2,1,0:T(8,128)(2,1)S(1)}, u32[]{:S(2)}, u32[]{:S(2)}) async-start(bf16[16,128,256]{2,1,0:T(8,128)(2,1)} %bitcast.67), calls=%async_computation.1 | async-start | bytes 2097152 | tf_op jit(solution)/shard_map/all_to_all | solution.py:372
  36.8 0.0 collective-permute-done.other
  36.8 0.0 copy-done.1
  36.8 0.0 copy-done.2
  36.8 0.0 copy-done.3
  36.8 0.0 copy-done.4
  36.8 12.6 %ssm.1.y = f32[16,128,256]{2,1,0:T(8,128)} custom-call(bf16[16,200,256]{2,1,0:T(8,128)(2,1)S(1)} %all-to-all-done.buf, bf16[16,64,256]{2,1,0:T(8,128)(2,1)S(1)} %collective-permute-done.other, f32[2,4,4224]{2,1,0:T(4,128)S(1)} %copy-done.1, f32[2,4224]{1,0:T(2,128)S(1)} %copy-done.2, f32[2,64]{1,0:T(2,128)S(1)} %copy-done.3, f32[2,64]{1,0:T(2,128)S(1)} %copy-done.4), custom_call_target="tpu_custom_call" | custom-call | flops 20000000000 | bytes 8388608 | tf_op jit(solution)/shard_map/ssm/pallas_call | solution.py:410
  49.5 1.7 %all-to-all-done.1.gate = bf16[16,128,256]{2,1,0:T(8,128)(2,1)S(1)} async-done(((bf16[16,128,256]{2,1,0:T(8,128)(2,1)}), bf16[16,128,256]{2,1,0:T(8,128)(2,1)S(1)}, u32[]{:S(2)}, u32[]{:S(2)}) %all-to-all-start.1) | async-done | bytes 1048608 | tf_op jit(solution)/shard_map/all_to_all | solution.py:372
  51.1 2.8 %gate.1 = (bf16[16,128,256]{2,1,0:T(8,128)(2,1)}, f32[16,128]{1,0:T(8,128)S(1)}) custom-call(f32[16,128,256]{2,1,0:T(8,128)} %ssm.1.y, bf16[16,128,256]{2,1,0:T(8,128)(2,1)S(1)} %all-to-all-done.1.gate), custom_call_target="tpu_custom_call" | custom-call | tf_op jit(solution)/shard_map/gate/pallas_call | solution.py:434
  53.9 0.0 copy-start
  53.9 3.4 %collective-permute-start.1 = (f32[2,4,128]{2,1,0:T(4,128)S(1)}, f32[2,4,128]{2,1,0:T(4,128)S(1)}, u32[]{:S(2)}, u32[]{:S(2)}) collective-permute-start(f32[2,4,128]{2,1,0:T(4,128)S(1)} %fusion.2), channel_id=1, source_target_pairs={{0,4},{1,5},{2,6},{3,7},{4,0},{5,1},{6,2},{7,3},{8,12},{9,13},{10,... | collective-permute-start | bytes 12296 | tf_op jit(solution)/shard_map/ppermute | solution.py:357
  57.3 1.6 %collective-permute-done.1 = f32[2,4,128]{2,1,0:T(4,128)S(1)} collective-permute-done((f32[2,4,128]{2,1,0:T(4,128)S(1)}, f32[2,4,128]{2,1,0:T(4,128)S(1)}, u32[]{:S(2)}, u32[]{:S(2)}) %collective-permute-start.1) | collective-permute-done | bytes 4128 | tf_op jit(solution)/shard_map/ppermute | solution.py:357
  58.9 0.1 collective-permute-start.2
  59.0 0.5 collective-permute-start.3
  59.5 1.3 %collective-permute-start.4 = (f32[16,128]{1,0:T(8,128)S(1)}, f32[16,128]{1,0:T(8,128)S(1)}, u32[]{:S(2)}, u32[]{:S(2)}) collective-permute-start(f32[16,128]{1,0:T(8,128)S(1)} %bitcast.81), channel_id=1, source_target_pairs={{0,48},{16,32},{32,16},{48,0},{64,112},{80,96},{96,80},{112,64},{1... | collective-permute-start | bytes 24584 | tf_op jit(solution)/shard_map/ppermute | solution.py:346
  60.8 0.0 collective-permute-done.2
  60.8 1.9 %collective-permute-done.3 = f32[16,128]{1,0:T(8,128)S(1)} collective-permute-done((f32[16,128]{1,0:T(8,128)S(1)}, f32[16,128]{1,0:T(8,128)S(1)}, u32[]{:S(2)}, u32[]{:S(2)}) %collective-permute-start.3) | collective-permute-done | bytes 8224 | tf_op jit(solution)/shard_map/ppermute | solution.py:346
  62.7 0.0 collective-permute-done.4
  62.7 1.8 %collective-permute-start.5 = (f32[16,128]{1,0:T(8,128)S(1)}, f32[16,128]{1,0:T(8,128)S(1)}, u32[]{:S(2)}, u32[]{:S(2)}) collective-permute-start(f32[16,128]{1,0:T(8,128)S(1)} %add_add_fusion.1), channel_id=1, source_target_pairs={{0,64},{16,80},{32,96},{48,112},{64,128},{80,144},{96,160},{112,17... | collective-permute-start | bytes 24584 | tf_op jit(solution)/shard_map/ppermute | solution.py:346
  64.6 2.5 %collective-permute-start.6 = (f32[16,128]{1,0:T(8,128)S(1)}, f32[16,128]{1,0:T(8,128)S(1)}, u32[]{:S(2)}, u32[]{:S(2)}) collective-permute-start(f32[16,128]{1,0:T(8,128)S(1)} %add_add_fusion.1), channel_id=1, source_target_pairs={{0,128},{16,144},{32,160},{48,176},{64,192},{80,208},{96,224},{112... | collective-permute-start | bytes 24584 | tf_op jit(solution)/shard_map/ppermute | solution.py:346
  67.1 0.3 collective-permute-start.7
  67.4 10.6 %all-to-all-start.2 = ((bf16[16,128,256]{2,1,0:T(8,128)(2,1)}), bf16[16,128,256]{2,1,0:T(8,128)(2,1)S(1)}, u32[]{:S(2)}, u32[]{:S(2)}) async-start(bf16[16,128,256]{2,1,0:T(8,128)(2,1)} %get-tuple-element.11), calls=%async_computation.2 | async-start | bytes 2097152 | tf_op jit(solution)/shard_map/all_to_all | solution.py:372
  78.0 0.0 collective-permute-done.5
  78.0 0.0 collective-permute-done.6
  78.0 0.0 collective-permute-done.7
  78.1 3.5 %collective-permute-start.8 = (f32[8,1,128]{2,0,1:T(8,128)S(1)}, f32[8,1,128]{2,0,1:T(8,128)S(1)}, u32[]{:S(2)}, u32[]{:S(2)}) collective-permute-start(f32[8,1,128]{2,0,1:T(8,128)S(1)} %broadcast_select_fusion.2), channel_id=1, source_target_pairs={{0,1},{1,0},{2,3},{3,2},{4,5},{5,4},{6,7},{7,6},{8,9},{9,8},{10,11... | collective-permute-start | bytes 12296 | tf_op jit(solution)/shard_map/ppermute | solution.py:357
  81.6 2.3 %collective-permute-done.8 = f32[8,1,128]{2,0,1:T(8,128)S(1)} collective-permute-done((f32[8,1,128]{2,0,1:T(8,128)S(1)}, f32[8,1,128]{2,0,1:T(8,128)S(1)}, u32[]{:S(2)}, u32[]{:S(2)}) %collective-permute-start.8) | collective-permute-done | bytes 4128 | tf_op jit(solution)/shard_map/ppermute | solution.py:357
  83.9 1.6 %collective-permute-start.9 = (f32[4,2,128]{2,0,1:T(4,128)S(1)}, f32[4,2,128]{2,0,1:T(4,128)S(1)}, u32[]{:S(2)}, u32[]{:S(2)}) collective-permute-start(f32[4,2,128]{2,0,1:T(4,128)S(1)} %bitcast.86), channel_id=1, source_target_pairs={{0,2},{1,3},{2,0},{3,1},{4,6},{5,7},{6,4},{7,5},{8,10},{9,11},{10,... | collective-permute-start | bytes 12296 | tf_op jit(solution)/shard_map/ppermute | solution.py:357
  85.5 16.3 %collective-permute-done.9 = f32[4,2,128]{2,0,1:T(4,128)S(1)} collective-permute-done((f32[4,2,128]{2,0,1:T(4,128)S(1)}, f32[4,2,128]{2,0,1:T(4,128)S(1)}, u32[]{:S(2)}, u32[]{:S(2)}) %collective-permute-start.9) | collective-permute-done | bytes 4128 | tf_op jit(solution)/shard_map/ppermute | solution.py:357
  101.8 5.0 %collective-permute-start.10 = (f32[1,8,128]{2,1,0:T(8,128)S(1)}, f32[1,8,128]{2,1,0:T(8,128)S(1)}, u32[]{:S(2)}, u32[]{:S(2)}) collective-permute-start(f32[1,8,128]{2,1,0:T(8,128)S(1)} %fusion.1), channel_id=1, source_target_pairs={{0,8},{1,9},{2,10},{3,11},{4,12},{5,13},{6,14},{7,15},{8,0},{9,1},... | collective-permute-start | bytes 12296 | tf_op jit(solution)/shard_map/ppermute | solution.py:357
  106.8 2.6 %collective-permute-done.10 = f32[1,8,128]{2,1,0:T(8,128)S(1)} collective-permute-done((f32[1,8,128]{2,1,0:T(8,128)S(1)}, f32[1,8,128]{2,1,0:T(8,128)S(1)}, u32[]{:S(2)}, u32[]{:S(2)}) %collective-permute-start.10) | collective-permute-done | bytes 4128 | tf_op jit(solution)/shard_map/ppermute | solution.py:357
  109.4 0.0 all-to-all-done.2.gated
  109.4 0.0 copy-done
  109.4 1.3 %norm.1 = bf16[16,128,256]{2,1,0:T(8,128)(2,1)} custom-call(bf16[16,128,256]{2,1,0:T(8,128)(2,1)S(1)} %all-to-all-done.2.gated, f32[16,128]{1,0:T(8,128)S(1)} %maximum_bitcast_fusion.total, f32[1,4096]{1,0:T(1,128)S(1)} %bitcast.66), custom_call_target="tpu_custom_call" | custom-call | tf_op jit(solution)/shard_map/norm/pallas_call | solution.py:456
  (16 shorter events, 0.1 us)
Async XLA Ops:
  2.8 26.8 %all-to-all-start = ((bf16[16,200,256]{2,1,0:T(8,128)(2,1)}), bf16[16,200,256]{2,1,0:T(8,128)(2,1)S(1)}, u32[]{:S(2)}, u32[]{:S(2)}) async-start(bf16[16,200,256]{2,1,0:T(8,128)(2,1)} %pack.1), calls=%async_computation | async-start | bytes 3276800 | tf_op jit(solution)/shard_map/all_to_all | solution.py:372
  11.6 25.2 %copy-start.1 = (f32[2,4,4224]{2,1,0:T(4,128)S(1)}, f32[2,4,4224]{2,1,0:T(4,128)}, u32[]{:S(2)}) copy-start(f32[2,4,4224]{2,1,0:T(4,128)} %cw.1) | copy-start | bytes 405508
  11.6 25.2 %copy-start.2 = (f32[2,4224]{1,0:T(2,128)S(1)}, f32[2,4224]{1,0:T(2,128)}, u32[]{:S(2)}) copy-start(f32[2,4224]{1,0:T(2,128)} %cb.1) | copy-start | bytes 101380
  11.6 25.2 %copy-start.3 = (f32[2,64]{1,0:T(2,128)S(1)}, f32[2,64]{1,0:T(2,128)}, u32[]{:S(2)}) copy-start(f32[2,64]{1,0:T(2,128)} %rate.1) | copy-start | bytes 1540
  11.6 25.2 %copy-start.4 = (f32[2,64]{1,0:T(2,128)S(1)}, f32[2,64]{1,0:T(2,128)}, u32[]{:S(2)}) copy-start(f32[2,64]{1,0:T(2,128)} %skip.1) | copy-start | bytes 1540
  30.5 6.3 %collective-permute-start = (bf16[16,64,256]{2,1,0:T(8,128)(2,1)}, bf16[16,64,256]{2,1,0:T(8,128)(2,1)S(1)}, u32[]{:S(2)}, u32[]{:S(2)}) collective-permute-start(bf16[16,64,256]{2,1,0:T(8,128)(2,1)} %slice.35), channel_id=1, source_target_pairs={{0,16},{16,0},{32,48},{48,32},{64,80},{80,64},{96,112},{112,96},{1... | collective-permute-start | bytes 1572872 | tf_op jit(solution)/shard_map/ppermute | solution.py:406
  30.5 20.6 %all-to-all-start.1 = ((bf16[16,128,256]{2,1,0:T(8,128)(2,1)}), bf16[16,128,256]{2,1,0:T(8,128)(2,1)S(1)}, u32[]{:S(2)}, u32[]{:S(2)}) async-start(bf16[16,128,256]{2,1,0:T(8,128)(2,1)} %bitcast.67), calls=%async_computation.1 | async-start | bytes 2097152 | tf_op jit(solution)/shard_map/all_to_all | solution.py:372
  53.9 55.5 %copy-start = (f32[4096]{0:T(1024)S(1)}, f32[4096]{0:T(1024)}, u32[]{:S(2)}) copy-start(f32[4096]{0:T(1024)} %param.19) | copy-start | bytes 49156
  53.9 4.9 %collective-permute-start.1 = (f32[2,4,128]{2,1,0:T(4,128)S(1)}, f32[2,4,128]{2,1,0:T(4,128)S(1)}, u32[]{:S(2)}, u32[]{:S(2)}) collective-permute-start(f32[2,4,128]{2,1,0:T(4,128)S(1)} %fusion.2), channel_id=1, source_target_pairs={{0,4},{1,5},{2,6},{3,7},{4,0},{5,1},{6,2},{7,3},{8,12},{9,13},{10,... | collective-permute-start | bytes 12296 | tf_op jit(solution)/shard_map/ppermute | solution.py:357
  58.9 2.0 %collective-permute-start.2 = (f32[16,128]{1,0:T(8,128)S(1)}, f32[16,128]{1,0:T(8,128)S(1)}, u32[]{:S(2)}, u32[]{:S(2)}) collective-permute-start(f32[16,128]{1,0:T(8,128)S(1)} %bitcast.79), channel_id=1, source_target_pairs={{0,16},{16,0},{32,48},{48,32},{64,80},{80,64},{96,112},{112,96},{1... | collective-permute-start | bytes 24584 | tf_op jit(solution)/shard_map/ppermute | solution.py:346
  59.0 3.7 %collective-permute-start.3 = (f32[16,128]{1,0:T(8,128)S(1)}, f32[16,128]{1,0:T(8,128)S(1)}, u32[]{:S(2)}, u32[]{:S(2)}) collective-permute-start(f32[16,128]{1,0:T(8,128)S(1)} %bitcast.80), channel_id=1, source_target_pairs={{0,32},{16,48},{32,0},{48,16},{64,96},{80,112},{96,64},{112,80},{1... | collective-permute-start | bytes 24584 | tf_op jit(solution)/shard_map/ppermute | solution.py:346
  59.5 3.2 %collective-permute-start.4 = (f32[16,128]{1,0:T(8,128)S(1)}, f32[16,128]{1,0:T(8,128)S(1)}, u32[]{:S(2)}, u32[]{:S(2)}) collective-permute-start(f32[16,128]{1,0:T(8,128)S(1)} %bitcast.81), channel_id=1, source_target_pairs={{0,48},{16,32},{32,16},{48,0},{64,112},{80,96},{96,80},{112,64},{1... | collective-permute-start | bytes 24584 | tf_op jit(solution)/shard_map/ppermute | solution.py:346
  62.7 15.3 %collective-permute-start.5 = (f32[16,128]{1,0:T(8,128)S(1)}, f32[16,128]{1,0:T(8,128)S(1)}, u32[]{:S(2)}, u32[]{:S(2)}) collective-permute-start(f32[16,128]{1,0:T(8,128)S(1)} %add_add_fusion.1), channel_id=1, source_target_pairs={{0,64},{16,80},{32,96},{48,112},{64,128},{80,144},{96,160},{112,17... | collective-permute-start | bytes 24584 | tf_op jit(solution)/shard_map/ppermute | solution.py:346
  64.6 13.4 %collective-permute-start.6 = (f32[16,128]{1,0:T(8,128)S(1)}, f32[16,128]{1,0:T(8,128)S(1)}, u32[]{:S(2)}, u32[]{:S(2)}) collective-permute-start(f32[16,128]{1,0:T(8,128)S(1)} %add_add_fusion.1), channel_id=1, source_target_pairs={{0,128},{16,144},{32,160},{48,176},{64,192},{80,208},{96,224},{112... | collective-permute-start | bytes 24584 | tf_op jit(solution)/shard_map/ppermute | solution.py:346
  67.1 10.9 %collective-permute-start.7 = (f32[16,128]{1,0:T(8,128)S(1)}, f32[16,128]{1,0:T(8,128)S(1)}, u32[]{:S(2)}, u32[]{:S(2)}) collective-permute-start(f32[16,128]{1,0:T(8,128)S(1)} %add_add_fusion.1), channel_id=1, source_target_pairs={{0,192},{16,208},{32,224},{48,240},{64,0},{80,16},{96,32},{112,48}... | collective-permute-start | bytes 24584 | tf_op jit(solution)/shard_map/ppermute | solution.py:346
  67.4 42.0 %all-to-all-start.2 = ((bf16[16,128,256]{2,1,0:T(8,128)(2,1)}), bf16[16,128,256]{2,1,0:T(8,128)(2,1)S(1)}, u32[]{:S(2)}, u32[]{:S(2)}) async-start(bf16[16,128,256]{2,1,0:T(8,128)(2,1)} %get-tuple-element.11), calls=%async_computation.2 | async-start | bytes 2097152 | tf_op jit(solution)/shard_map/all_to_all | solution.py:372
  78.1 5.8 %collective-permute-start.8 = (f32[8,1,128]{2,0,1:T(8,128)S(1)}, f32[8,1,128]{2,0,1:T(8,128)S(1)}, u32[]{:S(2)}, u32[]{:S(2)}) collective-permute-start(f32[8,1,128]{2,0,1:T(8,128)S(1)} %broadcast_select_fusion.2), channel_id=1, source_target_pairs={{0,1},{1,0},{2,3},{3,2},{4,5},{5,4},{6,7},{7,6},{8,9},{9,8},{10,11... | collective-permute-start | bytes 12296 | tf_op jit(solution)/shard_map/ppermute | solution.py:357
  83.9 17.8 %collective-permute-start.9 = (f32[4,2,128]{2,0,1:T(4,128)S(1)}, f32[4,2,128]{2,0,1:T(4,128)S(1)}, u32[]{:S(2)}, u32[]{:S(2)}) collective-permute-start(f32[4,2,128]{2,0,1:T(4,128)S(1)} %bitcast.86), channel_id=1, source_target_pairs={{0,2},{1,3},{2,0},{3,1},{4,6},{5,7},{6,4},{7,5},{8,10},{9,11},{10,... | collective-permute-start | bytes 12296 | tf_op jit(solution)/shard_map/ppermute | solution.py:357
  101.8 7.6 %collective-permute-start.10 = (f32[1,8,128]{2,1,0:T(8,128)S(1)}, f32[1,8,128]{2,1,0:T(8,128)S(1)}, u32[]{:S(2)}, u32[]{:S(2)}) collective-permute-start(f32[1,8,128]{2,1,0:T(8,128)S(1)} %fusion.1), channel_id=1, source_target_pairs={{0,8},{1,9},{2,10},{3,11},{4,12},{5,13},{6,14},{7,15},{8,0},{9,1},... | collective-permute-start | bytes 12296 | tf_op jit(solution)/shard_map/ppermute | solution.py:357
where the time goes:
time: 112 us; the launch traced here: 111 us
  waiting for transfers between devices  44.4 us (40%)
  starting transfers between devices  42.7 us (38%)
  Pallas kernels  19.5 us (17%)
  local copies, waits for them, and re-layouts  3.82 us (3%)
    ppermute x4, waiting for transfers between devices, turned_over(): got = lax.ppermute(give, 'batch', [(i, i ^ 1 << b) for i in range(BLOCKS)])  22.8 us
    all_to_all x3, starting transfers between devices, swap(): return lax.all_to_all(array, axis, split_axis=0, concat_axis=0, tiled=True)  22.7 us
    all_to_all x3, waiting for transfers between devices, swap(): return lax.all_to_all(array, axis, split_axis=0, concat_axis=0, tiled=True)  19.7 us
    ppermute x4, starting transfers between devices, turned_over(): got = lax.ppermute(give, 'batch', [(i, i ^ 1 << b) for i in range(BLOCKS)])  13.4 us
    pallas_call x1, Pallas kernels, shards(): pl.pallas_call(ssm_kernel, out_shape=pltpu.HBM((BLOCKS, GROUP, WIDE), f32...  12.6 us
    ppermute x6, starting transfers between devices, total_of(): came = [lax.ppermute(sums, 'tm', list(enumerate(move))) for move in moves]  6.63 us
    pallas_call x1, Pallas kernels, shards(): pl.pallas_call(pack_kernel, out_shape=pltpu.HBM((BLOCKS, ROWS, WIDE), bf1...  2.81 us
    pallas_call x1, Pallas kernels, shards(): pl.pallas_call(gate_kernel, out_shape=(pltpu.HBM((BLOCKS, GROUP, WIDE), b...  2.77 us
  transfers between devices with their start and end apart: 14, of which 7 were waited for; matrix products, arithmetic and copies ran while one was open for 3% of the time, Pallas kernels for 11%

commit v1 on v0

--- a/solution.py
+++ b/solution.py
@@ -324,17 +324,17 @@
     columns = jnp.concatenate([inv, jnp.zeros((GROUP - BLOCKS, GROUP), jnp.float32)], axis=0).T
 
     def send(j):
-        at = pl.ds(j * 4, 4)
+        at = pl.ds(j * 2, 2)
         return pltpu.make_async_copy(out.at[at], target.at[at], sent.at[j])
 
-    for j in range(BLOCKS // 4):
+    for j in range(BLOCKS // 2):
         if j > 0:
             send(j - 1).start()
-        for i in range(4 * j, 4 * j + 4):
+        for i in range(2 * j, 2 * j + 2):
             wide = gated[i].astype(jnp.float32) * columns[:, i : i + 1] * gains
             out[i] = wide.astype(jnp.bfloat16)
-    send(BLOCKS // 4 - 1).start()
-    for j in range(BLOCKS // 4):
+    send(BLOCKS // 2 - 1).start()
+    for j in range(BLOCKS // 2):
         send(j).wait()
 
 
@@ -460,7 +460,7 @@
         out_specs=ANY,
         scratch_shapes=[
             pltpu.VMEM((BLOCKS, GROUP, WIDE), bf16),
-            pltpu.SemaphoreType.DMA((BLOCKS // 4,)),
+            pltpu.SemaphoreType.DMA((BLOCKS // 2,)),
         ],
         compiler_params=LIMIT,
         name="norm",

time: 112 us -> 112 us (level)
  no operation moved by 1% of the time
where the time goes in v1:
time: 112 us; the launch traced here: 111 us
  waiting for transfers between devices  44.4 us (40%)
  starting transfers between devices  42.7 us (38%)
  Pallas kernels  19.5 us (17%)
  local copies, waits for them, and re-layouts  3.82 us (3%)
    ppermute x4, waiting for transfers between devices, turned_over(): got = lax.ppermute(give, 'batch', [(i, i ^ 1 << b) for i in range(BLOCKS)])  22.8 us
    all_to_all x3, starting transfers between devices, swap(): return lax.all_to_all(array, axis, split_axis=0, concat_axis=0, tiled=True)  22.7 us
    all_to_all x3, waiting for transfers between devices, swap(): return lax.all_to_all(array, axis, split_axis=0, concat_axis=0, tiled=True)  19.7 us
    ppermute x4, starting transfers between devices, turned_over(): got = lax.ppermute(give, 'batch', [(i, i ^ 1 << b) for i in range(BLOCKS)])  13.4 us
    pallas_call x1, Pallas kernels, shards(): pl.pallas_call(ssm_kernel, out_shape=pltpu.HBM((BLOCKS, GROUP, WIDE), f32...  12.6 us
    ppermute x6, starting transfers between devices, total_of(): came = [lax.ppermute(sums, 'tm', list(enumerate(move))) for move in moves]  6.63 us
    pallas_call x1, Pallas kernels, shards(): pl.pallas_call(pack_kernel, out_shape=pltpu.HBM((BLOCKS, ROWS, WIDE), bf1...  2.81 us
    pallas_call x1, Pallas kernels, shards(): pl.pallas_call(gate_kernel, out_shape=(pltpu.HBM((BLOCKS, GROUP, WIDE), b...  2.77 us
  transfers between devices with their start and end apart: 14, of which 7 were waited for; matrix products, arithmetic and copies ran while one was open for 3% of the time, Pallas kernels for 11%

profile of v1, /device:TPU:2, one launch (start us, length us, event | category | flops | bytes accessed | tf_op | source)
XLA Modules:
  0.0 110.7 jit_solution(2217540466209796164)
XLA Ops:
  0.0 2.8 %pack.1 = bf16[16,200,256]{2,1,0:T(8,128)(2,1)} custom-call(bf16[1,128,4096]{2,1,0:T(8,128)(2,1)} %signal.1, bf16[1,128,128]{2,1,0:T(8,128)(2,1)} %bcf.1, bf16[1,128,128]{2,1,0:T(8,128)(2,1)} %bcb.1, bf16[1,128,128]{2,1,0:T(8,128)(2,1)} %step.1), custom_call_target="tpu_custom_call" | custom-call | bytes 3145728 | tf_op jit(solution)/shard_map/pack/pallas_call | solution.py:388
  2.8 5.9 %all-to-all-start = ((bf16[16,200,256]{2,1,0:T(8,128)(2,1)}), bf16[16,200,256]{2,1,0:T(8,128)(2,1)S(1)}, u32[]{:S(2)}, u32[]{:S(2)}) async-start(bf16[16,200,256]{2,1,0:T(8,128)(2,1)} %pack.1), calls=%async_computation | async-start | bytes 3276800 | tf_op jit(solution)/shard_map/all_to_all | solution.py:372
  8.7 1.6 %copy.20 = bf16[1,128,4096]{1,2,0:T(8,128)(2,1)S(1)} copy(bf16[1,128,4096]{2,1,0:T(8,128)(2,1)} %param.11) | data formatting | bytes 2097152 | tf_op args[1]
  10.3 1.3 %copy.21 = bf16[128,16,256]{2,0,1:T(8,128)(2,1)} copy(bf16[128,16,256]{0,2,1:T(8,128)(2,1)S(1)} %bitcast.68) | data formatting | bytes 2097152 | tf_op jit(solution)/shard_map/reshape;squeeze | solution.py:404
  11.6 0.0 copy-start.1
  11.6 0.0 copy-start.2
  11.6 0.0 copy-start.3
  11.6 0.0 copy-start.4
  11.6 18.0 %all-to-all-done.buf = bf16[16,200,256]{2,1,0:T(8,128)(2,1)S(1)} async-done(((bf16[16,200,256]{2,1,0:T(8,128)(2,1)}), bf16[16,200,256]{2,1,0:T(8,128)(2,1)S(1)}, u32[]{:S(2)}, u32[]{:S(2)}) %all-to-all-start) | async-done | bytes 1638432 | tf_op jit(solution)/shard_map/all_to_all | solution.py:372
  29.7 0.9 slice.35
  30.5 0.0 collective-permute-start
  30.5 6.3 %all-to-all-start.1 = ((bf16[16,128,256]{2,1,0:T(8,128)(2,1)}), bf16[16,128,256]{2,1,0:T(8,128)(2,1)S(1)}, u32[]{:S(2)}, u32[]{:S(2)}) async-start(bf16[16,128,256]{2,1,0:T(8,128)(2,1)} %bitcast.67), calls=%async_computation.1 | async-start | bytes 2097152 | tf_op jit(solution)/shard_map/all_to_all | solution.py:372
  36.8 0.0 collective-permute-done.other
  36.8 0.0 copy-done.1
  36.8 0.0 copy-done.2
  36.8 0.0 copy-done.3
  36.8 0.0 copy-done.4
  36.8 12.6 %ssm.1.y = f32[16,128,256]{2,1,0:T(8,128)} custom-call(bf16[16,200,256]{2,1,0:T(8,128)(2,1)S(1)} %all-to-all-done.buf, bf16[16,64,256]{2,1,0:T(8,128)(2,1)S(1)} %collective-permute-done.other, f32[2,4,4224]{2,1,0:T(4,128)S(1)} %copy-done.1, f32[2,4224]{1,0:T(2,128)S(1)} %copy-done.2, f32[2,64]{1,0:T(2,128)S(1)} %copy-done.3, f32[2,64]{1,0:T(2,128)S(1)} %copy-done.4), custom_call_target="tpu_custom_call" | custom-call | flops 20000000000 | bytes 8388608 | tf_op jit(solution)/shard_map/ssm/pallas_call | solution.py:410
  49.5 1.7 %all-to-all-done.1.gate = bf16[16,128,256]{2,1,0:T(8,128)(2,1)S(1)} async-done(((bf16[16,128,256]{2,1,0:T(8,128)(2,1)}), bf16[16,128,256]{2,1,0:T(8,128)(2,1)S(1)}, u32[]{:S(2)}, u32[]{:S(2)}) %all-to-all-start.1) | async-done | bytes 1048608 | tf_op jit(solution)/shard_map/all_to_all | solution.py:372
  51.1 2.8 %gate.1 = (bf16[16,128,256]{2,1,0:T(8,128)(2,1)}, f32[16,128]{1,0:T(8,128)S(1)}) custom-call(f32[16,128,256]{2,1,0:T(8,128)} %ssm.1.y, bf16[16,128,256]{2,1,0:T(8,128)(2,1)S(1)} %all-to-all-done.1.gate), custom_call_target="tpu_custom_call" | custom-call | tf_op jit(solution)/shard_map/gate/pallas_call | solution.py:434
  53.9 0.0 copy-start
  53.9 3.4 %collective-permute-start.1 = (f32[2,4,128]{2,1,0:T(4,128)S(1)}, f32[2,4,128]{2,1,0:T(4,128)S(1)}, u32[]{:S(2)}, u32[]{:S(2)}) collective-permute-start(f32[2,4,128]{2,1,0:T(4,128)S(1)} %fusion.2), channel_id=1, source_target_pairs={{0,4},{1,5},{2,6},{3,7},{4,0},{5,1},{6,2},{7,3},{8,12},{9,13},{10,... | collective-permute-start | bytes 12296 | tf_op jit(solution)/shard_map/ppermute | solution.py:357
  57.3 1.6 %collective-permute-done.1 = f32[2,4,128]{2,1,0:T(4,128)S(1)} collective-permute-done((f32[2,4,128]{2,1,0:T(4,128)S(1)}, f32[2,4,128]{2,1,0:T(4,128)S(1)}, u32[]{:S(2)}, u32[]{:S(2)}) %collective-permute-start.1) | collective-permute-done | bytes 4128 | tf_op jit(solution)/shard_map/ppermute | solution.py:357
  58.9 0.1 collective-permute-start.2
  59.0 0.5 collective-permute-start.3
  59.5 1.3 %collective-permute-start.4 = (f32[16,128]{1,0:T(8,128)S(1)}, f32[16,128]{1,0:T(8,128)S(1)}, u32[]{:S(2)}, u32[]{:S(2)}) collective-permute-start(f32[16,128]{1,0:T(8,128)S(1)} %bitcast.81), channel_id=1, source_target_pairs={{0,48},{16,32},{32,16},{48,0},{64,112},{80,96},{96,80},{112,64},{1... | collective-permute-start | bytes 24584 | tf_op jit(solution)/shard_map/ppermute | solution.py:346
  60.8 0.0 collective-permute-done.2
  60.8 1.9 %collective-permute-done.3 = f32[16,128]{1,0:T(8,128)S(1)} collective-permute-done((f32[16,128]{1,0:T(8,128)S(1)}, f32[16,128]{1,0:T(8,128)S(1)}, u32[]{:S(2)}, u32[]{:S(2)}) %collective-permute-start.3) | collective-permute-done | bytes 8224 | tf_op jit(solution)/shard_map/ppermute | solution.py:346
  62.7 0.0 collective-permute-done.4
  62.7 1.8 %collective-permute-start.5 = (f32[16,128]{1,0:T(8,128)S(1)}, f32[16,128]{1,0:T(8,128)S(1)}, u32[]{:S(2)}, u32[]{:S(2)}) collective-permute-start(f32[16,128]{1,0:T(8,128)S(1)} %add_add_fusion.1), channel_id=1, source_target_pairs={{0,64},{16,80},{32,96},{48,112},{64,128},{80,144},{96,160},{112,17... | collective-permute-start | bytes 24584 | tf_op jit(solution)/shard_map/ppermute | solution.py:346
  64.6 2.5 %collective-permute-start.6 = (f32[16,128]{1,0:T(8,128)S(1)}, f32[16,128]{1,0:T(8,128)S(1)}, u32[]{:S(2)}, u32[]{:S(2)}) collective-permute-start(f32[16,128]{1,0:T(8,128)S(1)} %add_add_fusion.1), channel_id=1, source_target_pairs={{0,128},{16,144},{32,160},{48,176},{64,192},{80,208},{96,224},{112... | collective-permute-start | bytes 24584 | tf_op jit(solution)/shard_map/ppermute | solution.py:346
  67.1 0.3 collective-permute-start.7
  67.4 10.6 %all-to-all-start.2 = ((bf16[16,128,256]{2,1,0:T(8,128)(2,1)}), bf16[16,128,256]{2,1,0:T(8,128)(2,1)S(1)}, u32[]{:S(2)}, u32[]{:S(2)}) async-start(bf16[16,128,256]{2,1,0:T(8,128)(2,1)} %get-tuple-element.11), calls=%async_computation.2 | async-start | bytes 2097152 | tf_op jit(solution)/shard_map/all_to_all | solution.py:372
  78.0 0.0 collective-permute-done.5
  78.0 0.0 collective-permute-done.6
  78.0 0.0 collective-permute-done.7
  78.1 3.5 %collective-permute-start.8 = (f32[8,1,128]{2,0,1:T(8,128)S(1)}, f32[8,1,128]{2,0,1:T(8,128)S(1)}, u32[]{:S(2)}, u32[]{:S(2)}) collective-permute-start(f32[8,1,128]{2,0,1:T(8,128)S(1)} %broadcast_select_fusion.2), channel_id=1, source_target_pairs={{0,1},{1,0},{2,3},{3,2},{4,5},{5,4},{6,7},{7,6},{8,9},{9,8},{10,11... | collective-permute-start | bytes 12296 | tf_op jit(solution)/shard_map/ppermute | solution.py:357
  81.6 2.3 %collective-permute-done.8 = f32[8,1,128]{2,0,1:T(8,128)S(1)} collective-permute-done((f32[8,1,128]{2,0,1:T(8,128)S(1)}, f32[8,1,128]{2,0,1:T(8,128)S(1)}, u32[]{:S(2)}, u32[]{:S(2)}) %collective-permute-start.8) | collective-permute-done | bytes 4128 | tf_op jit(solution)/shard_map/ppermute | solution.py:357
  83.9 1.6 %collective-permute-start.9 = (f32[4,2,128]{2,0,1:T(4,128)S(1)}, f32[4,2,128]{2,0,1:T(4,128)S(1)}, u32[]{:S(2)}, u32[]{:S(2)}) collective-permute-start(f32[4,2,128]{2,0,1:T(4,128)S(1)} %bitcast.86), channel_id=1, source_target_pairs={{0,2},{1,3},{2,0},{3,1},{4,6},{5,7},{6,4},{7,5},{8,10},{9,11},{10,... | collective-permute-start | bytes 12296 | tf_op jit(solution)/shard_map/ppermute | solution.py:357
  85.5 16.3 %collective-permute-done.9 = f32[4,2,128]{2,0,1:T(4,128)S(1)} collective-permute-done((f32[4,2,128]{2,0,1:T(4,128)S(1)}, f32[4,2,128]{2,0,1:T(4,128)S(1)}, u32[]{:S(2)}, u32[]{:S(2)}) %collective-permute-start.9) | collective-permute-done | bytes 4128 | tf_op jit(solution)/shard_map/ppermute | solution.py:357
  101.8 5.0 %collective-permute-start.10 = (f32[1,8,128]{2,1,0:T(8,128)S(1)}, f32[1,8,128]{2,1,0:T(8,128)S(1)}, u32[]{:S(2)}, u32[]{:S(2)}) collective-permute-start(f32[1,8,128]{2,1,0:T(8,128)S(1)} %fusion.1), channel_id=1, source_target_pairs={{0,8},{1,9},{2,10},{3,11},{4,12},{5,13},{6,14},{7,15},{8,0},{9,1},... | collective-permute-start | bytes 12296 | tf_op jit(solution)/shard_map/ppermute | solution.py:357
  106.8 2.6 %collective-permute-done.10 = f32[1,8,128]{2,1,0:T(8,128)S(1)} collective-permute-done((f32[1,8,128]{2,1,0:T(8,128)S(1)}, f32[1,8,128]{2,1,0:T(8,128)S(1)}, u32[]{:S(2)}, u32[]{:S(2)}) %collective-permute-start.10) | collective-permute-done | bytes 4128 | tf_op jit(solution)/shard_map/ppermute | solution.py:357
  109.4 0.0 all-to-all-done.2.gated
  109.4 0.0 copy-done
  109.4 1.3 %norm.1 = bf16[16,128,256]{2,1,0:T(8,128)(2,1)} custom-call(bf16[16,128,256]{2,1,0:T(8,128)(2,1)S(1)} %all-to-all-done.2.gated, f32[16,128]{1,0:T(8,128)S(1)} %maximum_bitcast_fusion.total, f32[1,4096]{1,0:T(1,128)S(1)} %bitcast.66), custom_call_target="tpu_custom_call" | custom-call | tf_op jit(solution)/shard_map/norm/pallas_call | solution.py:456
  (16 shorter events, 0.1 us)
Async XLA Ops:
  2.8 26.8 %all-to-all-start = ((bf16[16,200,256]{2,1,0:T(8,128)(2,1)}), bf16[16,200,256]{2,1,0:T(8,128)(2,1)S(1)}, u32[]{:S(2)}, u32[]{:S(2)}) async-start(bf16[16,200,256]{2,1,0:T(8,128)(2,1)} %pack.1), calls=%async_computation | async-start | bytes 3276800 | tf_op jit(solution)/shard_map/all_to_all | solution.py:372
  11.6 25.2 %copy-start.1 = (f32[2,4,4224]{2,1,0:T(4,128)S(1)}, f32[2,4,4224]{2,1,0:T(4,128)}, u32[]{:S(2)}) copy-start(f32[2,4,4224]{2,1,0:T(4,128)} %cw.1) | copy-start | bytes 405508
  11.6 25.2 %copy-start.2 = (f32[2,4224]{1,0:T(2,128)S(1)}, f32[2,4224]{1,0:T(2,128)}, u32[]{:S(2)}) copy-start(f32[2,4224]{1,0:T(2,128)} %cb.1) | copy-start | bytes 101380
  11.6 25.2 %copy-start.3 = (f32[2,64]{1,0:T(2,128)S(1)}, f32[2,64]{1,0:T(2,128)}, u32[]{:S(2)}) copy-start(f32[2,64]{1,0:T(2,128)} %rate.1) | copy-start | bytes 1540
  11.6 25.2 %copy-start.4 = (f32[2,64]{1,0:T(2,128)S(1)}, f32[2,64]{1,0:T(2,128)}, u32[]{:S(2)}) copy-start(f32[2,64]{1,0:T(2,128)} %skip.1) | copy-start | bytes 1540
  30.5 6.3 %collective-permute-start = (bf16[16,64,256]{2,1,0:T(8,128)(2,1)}, bf16[16,64,256]{2,1,0:T(8,128)(2,1)S(1)}, u32[]{:S(2)}, u32[]{:S(2)}) collective-permute-start(bf16[16,64,256]{2,1,0:T(8,128)(2,1)} %slice.35), channel_id=1, source_target_pairs={{0,16},{16,0},{32,48},{48,32},{64,80},{80,64},{96,112},{112,96},{1... | collective-permute-start | bytes 1572872 | tf_op jit(solution)/shard_map/ppermute | solution.py:406
  30.5 20.6 %all-to-all-start.1 = ((bf16[16,128,256]{2,1,0:T(8,128)(2,1)}), bf16[16,128,256]{2,1,0:T(8,128)(2,1)S(1)}, u32[]{:S(2)}, u32[]{:S(2)}) async-start(bf16[16,128,256]{2,1,0:T(8,128)(2,1)} %bitcast.67), calls=%async_computation.1 | async-start | bytes 2097152 | tf_op jit(solution)/shard_map/all_to_all | solution.py:372
  53.9 55.5 %copy-start = (f32[4096]{0:T(1024)S(1)}, f32[4096]{0:T(1024)}, u32[]{:S(2)}) copy-start(f32[4096]{0:T(1024)} %param.19) | copy-start | bytes 49156
  53.9 4.9 %collective-permute-start.1 = (f32[2,4,128]{2,1,0:T(4,128)S(1)}, f32[2,4,128]{2,1,0:T(4,128)S(1)}, u32[]{:S(2)}, u32[]{:S(2)}) collective-permute-start(f32[2,4,128]{2,1,0:T(4,128)S(1)} %fusion.2), channel_id=1, source_target_pairs={{0,4},{1,5},{2,6},{3,7},{4,0},{5,1},{6,2},{7,3},{8,12},{9,13},{10,... | collective-permute-start | bytes 12296 | tf_op jit(solution)/shard_map/ppermute | solution.py:357
  58.9 2.0 %collective-permute-start.2 = (f32[16,128]{1,0:T(8,128)S(1)}, f32[16,128]{1,0:T(8,128)S(1)}, u32[]{:S(2)}, u32[]{:S(2)}) collective-permute-start(f32[16,128]{1,0:T(8,128)S(1)} %bitcast.79), channel_id=1, source_target_pairs={{0,16},{16,0},{32,48},{48,32},{64,80},{80,64},{96,112},{112,96},{1... | collective-permute-start | bytes 24584 | tf_op jit(solution)/shard_map/ppermute | solution.py:346
  59.0 3.7 %collective-permute-start.3 = (f32[16,128]{1,0:T(8,128)S(1)}, f32[16,128]{1,0:T(8,128)S(1)}, u32[]{:S(2)}, u32[]{:S(2)}) collective-permute-start(f32[16,128]{1,0:T(8,128)S(1)} %bitcast.80), channel_id=1, source_target_pairs={{0,32},{16,48},{32,0},{48,16},{64,96},{80,112},{96,64},{112,80},{1... | collective-permute-start | bytes 24584 | tf_op jit(solution)/shard_map/ppermute | solution.py:346
  59.5 3.2 %collective-permute-start.4 = (f32[16,128]{1,0:T(8,128)S(1)}, f32[16,128]{1,0:T(8,128)S(1)}, u32[]{:S(2)}, u32[]{:S(2)}) collective-permute-start(f32[16,128]{1,0:T(8,128)S(1)} %bitcast.81), channel_id=1, source_target_pairs={{0,48},{16,32},{32,16},{48,0},{64,112},{80,96},{96,80},{112,64},{1... | collective-permute-start | bytes 24584 | tf_op jit(solution)/shard_map/ppermute | solution.py:346
  62.7 15.3 %collective-permute-start.5 = (f32[16,128]{1,0:T(8,128)S(1)}, f32[16,128]{1,0:T(8,128)S(1)}, u32[]{:S(2)}, u32[]{:S(2)}) collective-permute-start(f32[16,128]{1,0:T(8,128)S(1)} %add_add_fusion.1), channel_id=1, source_target_pairs={{0,64},{16,80},{32,96},{48,112},{64,128},{80,144},{96,160},{112,17... | collective-permute-start | bytes 24584 | tf_op jit(solution)/shard_map/ppermute | solution.py:346
  64.6 13.4 %collective-permute-start.6 = (f32[16,128]{1,0:T(8,128)S(1)}, f32[16,128]{1,0:T(8,128)S(1)}, u32[]{:S(2)}, u32[]{:S(2)}) collective-permute-start(f32[16,128]{1,0:T(8,128)S(1)} %add_add_fusion.1), channel_id=1, source_target_pairs={{0,128},{16,144},{32,160},{48,176},{64,192},{80,208},{96,224},{112... | collective-permute-start | bytes 24584 | tf_op jit(solution)/shard_map/ppermute | solution.py:346
  67.1 10.9 %collective-permute-start.7 = (f32[16,128]{1,0:T(8,128)S(1)}, f32[16,128]{1,0:T(8,128)S(1)}, u32[]{:S(2)}, u32[]{:S(2)}) collective-permute-start(f32[16,128]{1,0:T(8,128)S(1)} %add_add_fusion.1), channel_id=1, source_target_pairs={{0,192},{16,208},{32,224},{48,240},{64,0},{80,16},{96,32},{112,48}... | collective-permute-start | bytes 24584 | tf_op jit(solution)/shard_map/ppermute | solution.py:346
  67.4 42.0 %all-to-all-start.2 = ((bf16[16,128,256]{2,1,0:T(8,128)(2,1)}), bf16[16,128,256]{2,1,0:T(8,128)(2,1)S(1)}, u32[]{:S(2)}, u32[]{:S(2)}) async-start(bf16[16,128,256]{2,1,0:T(8,128)(2,1)} %get-tuple-element.11), calls=%async_computation.2 | async-start | bytes 2097152 | tf_op jit(solution)/shard_map/all_to_all | solution.py:372
  78.1 5.8 %collective-permute-start.8 = (f32[8,1,128]{2,0,1:T(8,128)S(1)}, f32[8,1,128]{2,0,1:T(8,128)S(1)}, u32[]{:S(2)}, u32[]{:S(2)}) collective-permute-start(f32[8,1,128]{2,0,1:T(8,128)S(1)} %broadcast_select_fusion.2), channel_id=1, source_target_pairs={{0,1},{1,0},{2,3},{3,2},{4,5},{5,4},{6,7},{7,6},{8,9},{9,8},{10,11... | collective-permute-start | bytes 12296 | tf_op jit(solution)/shard_map/ppermute | solution.py:357
  83.9 17.8 %collective-permute-start.9 = (f32[4,2,128]{2,0,1:T(4,128)S(1)}, f32[4,2,128]{2,0,1:T(4,128)S(1)}, u32[]{:S(2)}, u32[]{:S(2)}) collective-permute-start(f32[4,2,128]{2,0,1:T(4,128)S(1)} %bitcast.86), channel_id=1, source_target_pairs={{0,2},{1,3},{2,0},{3,1},{4,6},{5,7},{6,4},{7,5},{8,10},{9,11},{10,... | collective-permute-start | bytes 12296 | tf_op jit(solution)/shard_map/ppermute | solution.py:357
  101.8 7.6 %collective-permute-start.10 = (f32[1,8,128]{2,1,0:T(8,128)S(1)}, f32[1,8,128]{2,1,0:T(8,128)S(1)}, u32[]{:S(2)}, u32[]{:S(2)}) collective-permute-start(f32[1,8,128]{2,1,0:T(8,128)S(1)} %fusion.1), channel_id=1, source_target_pairs={{0,8},{1,9},{2,10},{3,11},{4,12},{5,13},{6,14},{7,15},{8,0},{9,1},... | collective-permute-start | bytes 12296 | tf_op jit(solution)/shard_map/ppermute | solution.py:357
